TPU v7x, 512 devices: a whole 4x4x16 slice. The times are simulated.
512 devices in a mesh: aperture: 32 (over y, x, core), beam: 16 (over z).
Axes of the slice: x: 4, y: 4, z: 16, core: 2. Of those that a mesh axis runs over, the one named last changes fastest.
Arguments:
- subimages: bfloat16 [32, 2, 4096, 512], P('aperture', None, 'beam'), may hold values from -6 to 6
- range_kernel: bfloat16 [32, 2, 512, 512], P('aperture'), may hold values from -0.1875 to 0.1875
- weights0: bfloat16 [32, 64, 2, 128, 320], P('aperture', 'beam'), may hold values from -0.25 to 0.25
- starts0: int32 [32, 64], P(None, 'beam'), may hold values from -6 to 124, as said below
- weights1: bfloat16 [32, 128, 2, 128, 320], P('aperture', 'beam'), may hold values from -0.25 to 0.25
- starts1: int32 [32, 128], P(None, 'beam'), may hold values from -6 to 252, as said below
- owners: int32 [32, 256, 1], P('aperture', 'beam'), may hold values from 0 to 15; in each aligned block of 16 rows (0 to 15, 16 to 31, ..., all dimensions but the last counted through in order) at most 2 rows name the same one
Outputs:
- merged: bfloat16 [32, 512, 2, 64, 128], P('aperture', 'beam')
Inputs may be any that keep to these rules, and one draw needn't show every extreme that they name: starts0[s, p] = 2p - (10 - 2) // 2 + e with -2 <= e <= 2; both ends of e occur. starts1[s, p] = 2p - (10 - 2) // 2 + e with -2 <= e <= 2; both ends of e occur. `owners`: among the 16 sectors homed on one beam device (aligned blocks of 16 rows of one subaperture row), at most 2 name the same owner, a bound that some block reaches.
All inputs are finite; a program needn't handle non-finite values.
Results may differ from a plain program's by a relative error of at most 0.0072.
Values may be sent and summed in bfloat16 or wider, within the bound.
A program may use at most 64 MiB of HBM per device.

v0:
```python
import jax
import jax.numpy as jnp
from jax import lax
from jax.sharding import PartitionSpec as P

BLK = 32
NW = 10
REACH = 2
OS = 64


def extended(cells, sides, width):
    for axis, dim in sides:
        count = lax.axis_size(axis)
        ends = count - 1
        head = lax.slice_in_dim(cells, 0, width, axis=dim)
        tail = lax.slice_in_dim(cells, cells.shape[dim] - width, cells.shape[dim], axis=dim)
        cells = jnp.concatenate(
            [
                lax.ppermute(tail, axis, [(i, (i + 1) % count) for i in range(ends)]),
                cells,
                lax.ppermute(head, axis, [((i + 1) % count, i) for i in range(ends)]),
            ],
            axis=dim,
        )
    return cells


def partner(block, axis, distance):
    count = lax.axis_size(axis)
    route = []
    for low in range(count):
        high = low | 1 << distance
        if high != low and high < count:
            route += [(low, high), (high, low)]
    return lax.ppermute(block, axis, route)


def complex_dot(left_real, left_imag, right_real, right_imag):
    real_part = jnp.dot(left_real, right_real, preferred_element_type=jnp.float32) - jnp.dot(
        left_imag, right_imag, preferred_element_type=jnp.float32
    )
    imag_part = jnp.dot(left_real, right_imag, preferred_element_type=jnp.float32) + jnp.dot(
        left_imag, right_real, preferred_element_type=jnp.float32
    )
    return jnp.stack([real_part, imag_part])


def resample(subimage, kernel):
    return complex_dot(subimage[0], subimage[1], kernel[0], kernel[1]).astype(jnp.bfloat16)


def interpolate(padded, weights, starts, lowest_block):
    window_width = NW * BLK

    def cut_window(first_block):
        return lax.dynamic_slice_in_dim(padded, (first_block - lowest_block) * BLK, window_width, 1)

    windows = jax.vmap(cut_window)(starts)
    real_part = jnp.einsum(
        "npw,nwr->npr", weights[:, 0], windows[:, 0], preferred_element_type=jnp.float32
    ) - jnp.einsum("npw,nwr->npr", weights[:, 1], windows[:, 1], preferred_element_type=jnp.float32)
    imag_part = jnp.einsum(
        "npw,nwr->npr", weights[:, 0], windows[:, 1], preferred_element_type=jnp.float32
    ) + jnp.einsum("npw,nwr->npr", weights[:, 1], windows[:, 0], preferred_element_type=jnp.float32)
    stacked = jnp.stack([real_part, imag_part])
    return stacked.reshape(2, -1, padded.shape[2]).astype(jnp.bfloat16)


def table_row(table, row_number):
    return lax.dynamic_index_in_dim(table, row_number, 0, keepdims=False)


def range_part(array, part_index, part_width):
    return lax.dynamic_slice_in_dim(array, part_index * part_width, part_width, 2)


def local(subimages, range_kernel, weights0, starts0, weights1, starts1, owners):
    aper_index = lax.axis_index("aperture")
    beam_index = lax.axis_index("beam")
    halo_blocks = (NW - 2) // 2 + REACH
    margin = halo_blocks * BLK
    subimage = subimages[0]
    kernel = range_kernel[0]
    local_blocks = subimage.shape[1] // BLK
    source = resample(subimage, kernel)
    padded = extended(source, (("beam", 1),), margin)
    half_width = subimage.shape[2] // 2
    half_index = aper_index % 2
    lowest_first = beam_index * local_blocks - halo_blocks
    own_starts = table_row(starts0, aper_index)
    other_starts = table_row(starts0, jnp.bitwise_xor(aper_index, 1))
    own_half = range_part(padded, half_index, half_width)
    sent_half = range_part(padded, 1 - half_index, half_width)
    other_half, other_weights = partner((sent_half, weights0[0]), "aperture", 0)
    own_beams = interpolate(own_half, weights0[0], own_starts, lowest_first)
    other_beams = interpolate(other_half, other_weights, other_starts, lowest_first)
    level_one = (own_beams.astype(jnp.float32) + other_beams.astype(jnp.float32)).astype(
        jnp.bfloat16
    )
    padded_one = extended(level_one, (("beam", 1),), margin)
    quarter_width = half_width // 2
    quarter_index = aper_index // 2 % 2
    lowest_second = beam_index * (2 * local_blocks) - halo_blocks
    own_second = table_row(starts1, aper_index)
    other_second = table_row(starts1, jnp.bitwise_xor(aper_index, 2))
    own_quarter = range_part(padded_one, quarter_index, quarter_width)
    sent_quarter = range_part(padded_one, 1 - quarter_index, quarter_width)
    other_quarter, other_matrices = partner((sent_quarter, weights1[0]), "aperture", 1)
    own_final = interpolate(own_quarter, weights1[0], own_second, lowest_second)
    other_final = interpolate(other_quarter, other_matrices, other_second, lowest_second)
    quarter_piece = (own_final.astype(jnp.float32) + other_final.astype(jnp.float32)).astype(
        jnp.bfloat16
    )
    beam_count = lax.axis_size("beam")
    sector_count = owners.shape[1]
    capacity = max(2, 2 * sector_count // beam_count)
    per_sector = quarter_piece.reshape(2, sector_count, OS, quarter_width)
    target = owners[0, :, 0]
    one_hot = (target[:, None] == jnp.arange(beam_count, dtype=jnp.int32)[None, :]).astype(
        jnp.int32
    )
    earlier = jnp.cumsum(one_hot, axis=0) - one_hot
    slot_rank = jnp.sum(earlier * one_hot, axis=1)
    slot_index = target * capacity + slot_rank
    selector = (
        slot_index[None, :] == jnp.arange(beam_count * capacity, dtype=jnp.int32)[:, None]
    ).astype(jnp.bfloat16)
    outgoing = jnp.einsum(
        "so,copq->scpq", selector, per_sector, preferred_element_type=jnp.float32
    ).astype(jnp.bfloat16)
    received = lax.all_to_all(outgoing, "beam", split_axis=0, concat_axis=0, tiled=True)
    return received[None]


def solution(mesh):
    return jax.shard_map(
        local,
        mesh=mesh,
        in_specs=(
            P("aperture", None, "beam", None),
            P("aperture", None, None, None),
            P("aperture", "beam", None, None, None),
            P(None, "beam"),
            P("aperture", "beam", None, None, None),
            P(None, "beam"),
            P("aperture", "beam", None),
        ),
        out_specs=P("aperture", "beam", None, None, None),
        check_vma=False,
    )
```

profile of v0, /device:TPU:48, one launch (start us, length us, event | category | flops | bytes accessed | tf_op | source)
XLA Modules:
  0.0 162.5 jit_solution(941233120696847440)
XLA Ops:
  0.0 1.5 fusion.22
  1.6 1.2 fusion.26
  2.8 0.3 fusion.10
  3.1 0.3 fusion.11
  3.5 0.9 fusion.32
  4.4 3.8 %collective-permute-start = (bf16[2,192,512]{2,1,0:T(8,128)(2,1)}, bf16[2,192,512]{2,1,0:T(8,128)(2,1)S(1)}, u32[]{:S(2)}, u32[]{:S(2)}) collective-permute-start(bf16[2,192,512]{2,1,0:T(8,128)(2,1)} %get-tuple-element.23), channel_id=1, source_target_pairs={{0,1},{1,2},{2,3},{3,4},{4,5},{5,6},{6,7},{7,8},{8,9},{9,10},{10,1... | collective-permute-start | bytes 1179656 | tf_op jit(solution)/shard_map/ppermute | solution.py:20
  8.2 2.0 %collective-permute-start.1 = (bf16[2,192,512]{2,1,0:T(8,128)(2,1)}, bf16[2,192,512]{2,1,0:T(8,128)(2,1)S(1)}, u32[]{:S(2)}, u32[]{:S(2)}) collective-permute-start(bf16[2,192,512]{2,1,0:T(8,128)(2,1)} %get-tuple-element.24), channel_id=1, source_target_pairs={{1,0},{2,1},{3,2},{4,3},{5,4},{6,5},{7,6},{8,7},{9,8},{10,9},{11,1... | collective-permute-start | bytes 1179656 | tf_op jit(solution)/shard_map/ppermute | solution.py:22
  10.4 2.1 %collective-permute-start.3 = (bf16[4,2,128,320]{2,3,0,1:T(8,128)(2,1)S(1)}, bf16[4,2,128,320]{2,3,0,1:T(8,128)(2,1)}, u32[]{:S(2)}, u32[]{:S(2)}) collective-permute-start(bf16[4,2,128,320]{2,3,0,1:T(8,128)(2,1)S(1)} %bitcast.147), channel_id=1, source_target_pairs={{0,16},{16,0},{32,48},{48,32},{64,80},{80,64},{96,112},{112,96},{1... | collective-permute-start | bytes 1966088 | tf_op jit(solution)/shard_map/ppermute | solution.py:36
  12.5 3.4 %collective-permute-start.7 = (bf16[8,2,128,320]{2,3,0,1:T(8,128)(2,1)S(1)}, bf16[8,2,128,320]{2,3,0,1:T(8,128)(2,1)}, u32[]{:S(2)}, u32[]{:S(2)}) collective-permute-start(bf16[8,2,128,320]{2,3,0,1:T(8,128)(2,1)S(1)} %bitcast.142), channel_id=1, source_target_pairs={{0,32},{32,0},{16,48},{48,16},{64,96},{96,64},{80,112},{112,80},{1... | collective-permute-start | bytes 3932168 | tf_op jit(solution)/shard_map/ppermute | solution.py:36
  16.0 0.2 multiply_reduce_fusion.2
  16.4 0.2 select_reduce_fusion
  16.6 0.2 multiply_reduce_fusion
  16.8 0.5 collective-permute-done
  17.3 3.7 %collective-permute-done.1 = bf16[2,192,512]{2,1,0:T(8,128)(2,1)S(1)} collective-permute-done((bf16[2,192,512]{2,1,0:T(8,128)(2,1)}, bf16[2,192,512]{2,1,0:T(8,128)(2,1)S(1)}, u32[]{:S(2)}, u32[]{:S(2)}) %collective-permute-start.1) | collective-permute-done | bytes 393248 | tf_op jit(solution)/shard_map/ppermute | solution.py:22
  21.2 0.9 constant_dynamic-slice_fusion.2
  22.1 1.9 %collective-permute-start.2 = (bf16[2,640,256]{2,1,0:T(8,128)(2,1)}, bf16[2,640,256]{2,1,0:T(8,128)(2,1)}, u32[]{:S(2)}, u32[]{:S(2)}) collective-permute-start(bf16[2,640,256]{2,1,0:T(8,128)(2,1)} %get-tuple-element.15), channel_id=1, source_target_pairs={{0,16},{16,0},{32,48},{48,32},{64,80},{80,64},{96,112},{112,96},{1... | collective-permute-start | bytes 1966088 | tf_op jit(solution)/shard_map/ppermute | solution.py:36
  24.0 1.5 copy.29
  25.5 4.3 %gather_fusion = bf16[4,2,320,256]{3,1,2,0:T(2,128)(2,1)S(1)} fusion(bf16[2,640,256]{2,0,1:T(2,128)(2,1)} %copy.29, s32[4]{0:T(128)S(1)} %fusion.51), kind=kCustom, calls=%fused_computation | custom fusion | bytes 2621488 | tf_op jit(solution)/shard_map/vmap()/gather | solution.py:57
  29.8 1.8 %fusion.65 = (bf16[4,1,320,256]{3,1,2,0:T(2,128)(2,1)S(1)}, bf16[4,1,320,256]{3,1,2,0:T(2,128)(2,1)S(1)}) fusion(bf16[4,2,320,256]{3,1,2,0:T(2,128)(2,1)S(1)} %gather_fusion), kind=kLoop, calls=%fused_computation.120 | loop fusion | bytes 2621440 | tf_op jit(solution)/shard_map/slice | solution.py:61
  31.6 0.3 fusion.34
  32.0 0.3 fusion.6
  32.3 1.2 copy.33
  33.5 0.3 fusion.33
  33.9 0.3 fusion.7
  34.3 1.2 copy.34
  35.5 2.6 %copy.35 = bf16[2,640,256]{2,0,1:T(2,128)(2,1)} copy(bf16[2,640,256]{2,1,0:T(8,128)(2,1)} %collective-permute-done.2) | data formatting | bytes 1310720 | tf_op jit(solution)/shard_map/ppermute | solution.py:36
  38.1 4.3 %gather_fusion.1 = bf16[4,2,320,256]{3,1,2,0:T(2,128)(2,1)S(1)} fusion(bf16[2,640,256]{2,0,1:T(2,128)(2,1)} %copy.35, s32[4]{0:T(128)S(1)} %fusion.54), kind=kCustom, calls=%fused_computation.1 | custom fusion | bytes 2621488 | tf_op jit(solution)/shard_map/vmap()/gather | solution.py:57
  42.3 2.0 %fusion.64 = (bf16[4,1,320,256]{3,1,2,0:T(2,128)(2,1)S(1)}, bf16[4,1,320,256]{3,1,2,0:T(2,128)(2,1)S(1)}) fusion(bf16[4,2,320,256]{3,1,2,0:T(2,128)(2,1)S(1)} %gather_fusion.1), kind=kLoop, calls=%fused_computation.119 | loop fusion | bytes 2621440 | tf_op jit(solution)/shard_map/slice | solution.py:62
  44.4 1.3 fusion.36
  45.7 1.3 fusion.8
  47.0 0.4 copy.38
  47.4 1.3 fusion.35
  48.8 1.4 fusion.9
  50.2 0.4 copy.39
  50.6 2.2 %add_convert_fusion.1 = bf16[2,512,256]{2,0,1:T(2,128)(2,1)S(1)} fusion(bf16[1,512,256]{2,0,1:T(2,128)(2,1)S(1)} %copy-done.2, bf16[1,512,256]{2,0,1:T(2,128)(2,1)S(1)} %copy-done.1, bf16[1,512,256]{2,0,1:T(2,128)(2,1)S(1)} %copy.39, bf16[1,512,256]{2,0,1:T(2,128)(2,1)S(1)} %copy.38), kind=kLoop, calls=%fused_computation.30 | loop fusion | flops 2621440 | bytes 1572864 | tf_op jit(solution)/shard_map/convert_element_type | solution.py:98
  52.8 0.3 fusion.66
  53.1 5.1 %collective-permute-start.4 = (bf16[2,192,256]{2,0,1:T(2,128)(2,1)S(1)}, bf16[2,192,256]{2,0,1:T(2,128)(2,1)S(1)}, u32[]{:S(2)}, u32[]{:S(2)}) collective-permute-start(bf16[2,192,256]{2,0,1:T(2,128)(2,1)S(1)} %get-tuple-element.21), channel_id=1, source_target_pairs={{0,1},{1,2},{2,3},{3,4},{4,5},{5,6},{6,7},{7,8},{8,9},{9,10},{10,1... | collective-permute-start | bytes 589832 | tf_op jit(solution)/shard_map/ppermute | solution.py:20
  58.2 1.9 %collective-permute-start.5 = (bf16[2,192,256]{2,0,1:T(2,128)(2,1)S(1)}, bf16[2,192,256]{2,0,1:T(2,128)(2,1)S(1)}, u32[]{:S(2)}, u32[]{:S(2)}) collective-permute-start(bf16[2,192,256]{2,0,1:T(2,128)(2,1)S(1)} %get-tuple-element.22), channel_id=1, source_target_pairs={{1,0},{2,1},{3,2},{4,3},{5,4},{6,5},{7,6},{8,7},{9,8},{10,9},{11,1... | collective-permute-start | bytes 589832 | tf_op jit(solution)/shard_map/ppermute | solution.py:22
  60.1 2.9 %collective-permute-done.4 = bf16[2,192,256]{2,0,1:T(2,128)(2,1)S(1)} collective-permute-done((bf16[2,192,256]{2,0,1:T(2,128)(2,1)S(1)}, bf16[2,192,256]{2,0,1:T(2,128)(2,1)S(1)}, u32[]{:S(2)}, u32[]{:S(2)}) %collective-permute-start.4) | collective-permute-done | bytes 196640 | tf_op jit(solution)/shard_map/ppermute | solution.py:20
  63.0 5.3 %collective-permute-done.5 = bf16[2,192,256]{2,0,1:T(2,128)(2,1)S(1)} collective-permute-done((bf16[2,192,256]{2,0,1:T(2,128)(2,1)S(1)}, bf16[2,192,256]{2,0,1:T(2,128)(2,1)S(1)}, u32[]{:S(2)}, u32[]{:S(2)}) %collective-permute-start.5) | collective-permute-done | bytes 196640 | tf_op jit(solution)/shard_map/ppermute | solution.py:22
  68.3 1.3 pad_maximum_fusion.1
  69.6 1.4 constant_dynamic-slice_fusion
  71.0 3.6 %collective-permute-start.6 = (bf16[2,896,128]{2,0,1:T(2,128)(2,1)}, bf16[2,896,128]{2,0,1:T(2,128)(2,1)}, u32[]{:S(2)}, u32[]{:S(2)}) collective-permute-start(bf16[2,896,128]{2,0,1:T(2,128)(2,1)} %get-tuple-element.19), channel_id=1, source_target_pairs={{0,32},{32,0},{16,48},{48,16},{64,96},{96,64},{80,112},{112,80},{1... | collective-permute-start | bytes 1376264 | tf_op jit(solution)/shard_map/ppermute | solution.py:36
  74.6 3.2 %gather_fusion.2 = bf16[8,2,320,128]{3,1,2,0:T(2,128)(2,1)S(1)} fusion(bf16[2,896,128]{2,0,1:T(2,128)(2,1)S(1)} %get-tuple-element.20, s32[8]{0:T(128)S(1)} %fusion.57), kind=kCustom, calls=%fused_computation.2 | custom fusion | bytes 2621536 | tf_op jit(solution)/shard_map/vmap()/gather | solution.py:57
  77.8 2.4 %fusion.63 = (bf16[8,1,320,128]{3,1,2,0:T(2,128)(2,1)S(1)}, bf16[8,1,320,128]{3,1,2,0:T(2,128)(2,1)S(1)}) fusion(bf16[8,2,320,128]{3,1,2,0:T(2,128)(2,1)S(1)} %gather_fusion.2), kind=kLoop, calls=%fused_computation.118 | loop fusion | bytes 2621440 | tf_op jit(solution)/shard_map/slice | solution.py:61
  80.2 0.4 fusion.13
  80.6 0.4 fusion
  81.1 0.2 copy.43
  81.3 0.4 fusion.12
  81.7 0.4 fusion.1
  82.2 0.2 copy.44
  82.4 2.9 %collective-permute-done.6 = bf16[2,896,128]{2,0,1:T(2,128)(2,1)} collective-permute-done((bf16[2,896,128]{2,0,1:T(2,128)(2,1)}, bf16[2,896,128]{2,0,1:T(2,128)(2,1)}, u32[]{:S(2)}, u32[]{:S(2)}) %collective-permute-start.6) | collective-permute-done | bytes 458784 | tf_op jit(solution)/shard_map/ppermute | solution.py:36
  85.3 4.2 %gather_fusion.3 = bf16[8,2,320,128]{3,1,2,0:T(2,128)(2,1)S(1)} fusion(bf16[2,896,128]{2,0,1:T(2,128)(2,1)} %collective-permute-done.6, s32[8]{0:T(128)S(1)} %fusion.60), kind=kCustom, calls=%fused_computation.3 | custom fusion | bytes 2621536 | tf_op jit(solution)/shard_map/vmap()/gather | solution.py:57
  89.5 2.4 %fusion.62 = (bf16[8,1,320,128]{3,1,2,0:T(2,128)(2,1)S(1)}, bf16[8,1,320,128]{3,1,2,0:T(2,128)(2,1)S(1)}) fusion(bf16[8,2,320,128]{3,1,2,0:T(2,128)(2,1)S(1)} %gather_fusion.3), kind=kLoop, calls=%fused_computation.117 | loop fusion | bytes 2621440 | tf_op jit(solution)/shard_map/slice | solution.py:62
  91.9 1.5 fusion.15
  93.4 1.8 %fusion.2 = bf16[8,128,128]{1,2,0:T(8,128)(2,1)S(1)} fusion(f32[8,128,128]{1,2,0:T(8,128)S(1)} %fusion.15, bf16[8,2,128,320]{2,3,0,1:T(8,128)(2,1)} %collective-permute-done.7, bf16[8,1,320,128]{3,1,2,0:T(2,128)(2,1)S(1)} %get-tuple-element.10), kind=kOutput, calls=%fused_computation.19 | convolution fusion | flops 84148224 | bytes 2097152 | tf_op jit(solution)/shard_map/npw,nwr->npr/dot_general | solution.py:60
  95.2 0.2 copy.47
  95.4 1.5 fusion.14
  96.9 1.5 fusion.3
  98.5 0.2 copy.48
  98.7 0.5 convolution_convert_fusion
  99.2 0.4 copy.49
  99.6 61.9 %all_to_all.5 = bf16[32,2,64,128]{3,2,1,0:T(8,128)(2,1)S(1)} all-to-all(bf16[32,2,64,128]{3,2,1,0:T(8,128)(2,1)S(1)} %copy.49), channel_id=1, replica_groups=mesh['aperture'=32,'beam'=16] {'beam'}, dimensions={0} | all-to-all | bytes 2097152 | tf_op jit(solution)/shard_map/all_to_all | solution.py:132
  161.5 1.0 copy.88
  (31 shorter events, 0.4 us)
Async XLA Ops:
  0.0 1.5 copy-start
  0.0 2.8 %copy-start.3 = (bf16[1,2,256,512]{3,2,1,0:T(8,128)(2,1)S(1)}, bf16[1,2,256,512]{3,2,1,0:T(8,128)(2,1)}, u32[]{:S(2)}) copy-start(bf16[1,2,256,512]{3,2,1,0:T(8,128)(2,1)} %param.7) | copy-start | bytes 1572868
  3.1 7.1 %copy-start.5 = (bf16[1,4,2,128,320]{3,4,2,1,0:T(8,128)(2,1)S(1)}, bf16[1,4,2,128,320]{3,4,2,1,0:T(8,128)(2,1)}, u32[]{:S(2)}) copy-start(bf16[1,4,2,128,320]{3,4,2,1,0:T(8,128)(2,1)} %param.9) | copy-start | bytes 1966084
  3.4 9.0 %copy-start.4 = (bf16[1,8,2,128,320]{3,4,2,1,0:T(8,128)(2,1)S(1)}, bf16[1,8,2,128,320]{3,4,2,1,0:T(8,128)(2,1)}, u32[]{:S(2)}) copy-start(bf16[1,8,2,128,320]{3,4,2,1,0:T(8,128)(2,1)} %param.11) | copy-start | bytes 3932164
  4.4 12.9 %collective-permute-start = (bf16[2,192,512]{2,1,0:T(8,128)(2,1)}, bf16[2,192,512]{2,1,0:T(8,128)(2,1)S(1)}, u32[]{:S(2)}, u32[]{:S(2)}) collective-permute-start(bf16[2,192,512]{2,1,0:T(8,128)(2,1)} %get-tuple-element.23), channel_id=1, source_target_pairs={{0,1},{1,2},{2,3},{3,4},{4,5},{5,6},{6,7},{7,8},{8,9},{9,10},{10,1... | collective-permute-start | bytes 1179656 | tf_op jit(solution)/shard_map/ppermute | solution.py:20
  8.2 12.9 %collective-permute-start.1 = (bf16[2,192,512]{2,1,0:T(8,128)(2,1)}, bf16[2,192,512]{2,1,0:T(8,128)(2,1)S(1)}, u32[]{:S(2)}, u32[]{:S(2)}) collective-permute-start(bf16[2,192,512]{2,1,0:T(8,128)(2,1)} %get-tuple-element.24), channel_id=1, source_target_pairs={{1,0},{2,1},{3,2},{4,3},{5,4},{6,5},{7,6},{8,7},{9,8},{10,9},{11,1... | collective-permute-start | bytes 1179656 | tf_op jit(solution)/shard_map/ppermute | solution.py:22
  10.3 5.7 %copy-start.7 = (s32[32,4]{0,1:T(4,128)S(1)}, s32[32,4]{0,1:T(4,128)}, u32[]{:S(2)}) copy-start(s32[32,4]{0,1:T(4,128)} %param.10) | copy-start | bytes 1540
  10.3 5.9 %copy-start.8 = (s32[1,16,1]{1,2,0:T(1,128)S(1)}, s32[1,16,1]{1,2,0:T(1,128)}, u32[]{:S(2)}) copy-start(s32[1,16,1]{1,2,0:T(1,128)} %param.13) | copy-start | bytes 196
  10.3 6.2 %copy-start.6 = (s32[32,8]{0,1:T(8,128)S(1)}, s32[32,8]{0,1:T(8,128)}, u32[]{:S(2)}) copy-start(s32[32,8]{0,1:T(8,128)} %param.12) | copy-start | bytes 3076
  10.4 34.0 %collective-permute-start.3 = (bf16[4,2,128,320]{2,3,0,1:T(8,128)(2,1)S(1)}, bf16[4,2,128,320]{2,3,0,1:T(8,128)(2,1)}, u32[]{:S(2)}, u32[]{:S(2)}) collective-permute-start(bf16[4,2,128,320]{2,3,0,1:T(8,128)(2,1)S(1)} %bitcast.147), channel_id=1, source_target_pairs={{0,16},{16,0},{32,48},{48,32},{64,80},{80,64},{96,112},{112,96},{1... | collective-permute-start | bytes 1966088 | tf_op jit(solution)/shard_map/ppermute | solution.py:36
  12.5 79.4 %collective-permute-start.7 = (bf16[8,2,128,320]{2,3,0,1:T(8,128)(2,1)S(1)}, bf16[8,2,128,320]{2,3,0,1:T(8,128)(2,1)}, u32[]{:S(2)}, u32[]{:S(2)}) collective-permute-start(bf16[8,2,128,320]{2,3,0,1:T(8,128)(2,1)S(1)} %bitcast.142), channel_id=1, source_target_pairs={{0,32},{32,0},{16,48},{48,16},{64,96},{96,64},{80,112},{112,80},{1... | collective-permute-start | bytes 3932168 | tf_op jit(solution)/shard_map/ppermute | solution.py:36
  22.1 13.4 %collective-permute-start.2 = (bf16[2,640,256]{2,1,0:T(8,128)(2,1)}, bf16[2,640,256]{2,1,0:T(8,128)(2,1)}, u32[]{:S(2)}, u32[]{:S(2)}) collective-permute-start(bf16[2,640,256]{2,1,0:T(8,128)(2,1)} %get-tuple-element.15), channel_id=1, source_target_pairs={{0,16},{16,0},{32,48},{48,32},{64,80},{80,64},{96,112},{112,96},{1... | collective-permute-start | bytes 1966088 | tf_op jit(solution)/shard_map/ppermute | solution.py:36
  48.8 1.8 %copy-start.1 = (bf16[1,512,256]{2,0,1:T(2,128)(2,1)S(1)}, bf16[1,512,256]{2,0,1:T(2,128)(2,1)}, u32[]{:S(2)}) copy-start(bf16[1,512,256]{2,0,1:T(2,128)(2,1)} %copy.33) | copy-start | bytes 786436
  48.8 1.8 %copy-start.2 = (bf16[1,512,256]{2,0,1:T(2,128)(2,1)S(1)}, bf16[1,512,256]{2,0,1:T(2,128)(2,1)}, u32[]{:S(2)}) copy-start(bf16[1,512,256]{2,0,1:T(2,128)(2,1)} %copy.34) | copy-start | bytes 786436
  53.1 9.9 %collective-permute-start.4 = (bf16[2,192,256]{2,0,1:T(2,128)(2,1)S(1)}, bf16[2,192,256]{2,0,1:T(2,128)(2,1)S(1)}, u32[]{:S(2)}, u32[]{:S(2)}) collective-permute-start(bf16[2,192,256]{2,0,1:T(2,128)(2,1)S(1)} %get-tuple-element.21), channel_id=1, source_target_pairs={{0,1},{1,2},{2,3},{3,4},{4,5},{5,6},{6,7},{7,8},{8,9},{9,10},{10,1... | collective-permute-start | bytes 589832 | tf_op jit(solution)/shard_map/ppermute | solution.py:20
  58.2 10.1 %collective-permute-start.5 = (bf16[2,192,256]{2,0,1:T(2,128)(2,1)S(1)}, bf16[2,192,256]{2,0,1:T(2,128)(2,1)S(1)}, u32[]{:S(2)}, u32[]{:S(2)}) collective-permute-start(bf16[2,192,256]{2,0,1:T(2,128)(2,1)S(1)} %get-tuple-element.22), channel_id=1, source_target_pairs={{1,0},{2,1},{3,2},{4,3},{5,4},{6,5},{7,6},{8,7},{9,8},{10,9},{11,1... | collective-permute-start | bytes 589832 | tf_op jit(solution)/shard_map/ppermute | solution.py:22
  71.0 14.3 %collective-permute-start.6 = (bf16[2,896,128]{2,0,1:T(2,128)(2,1)}, bf16[2,896,128]{2,0,1:T(2,128)(2,1)}, u32[]{:S(2)}, u32[]{:S(2)}) collective-permute-start(bf16[2,896,128]{2,0,1:T(2,128)(2,1)} %get-tuple-element.19), channel_id=1, source_target_pairs={{0,32},{32,0},{16,48},{48,16},{64,96},{96,64},{80,112},{112,80},{1... | collective-permute-start | bytes 1376264 | tf_op jit(solution)/shard_map/ppermute | solution.py:36
where the time goes:
time: 163 us; the launch traced here: 162 us
  blocking collectives  61.9 us (38%)
  local copies, waits for them, and re-layouts  36.7 us (23%)
  starting transfers between devices  23.8 us (15%)
  matrix products  18.9 us (12%)
  waiting for transfers between devices  15.4 us (9%)
  other arithmetic  5.27 us (3%)
    all_to_all x1, blocking collectives, local(): lax.all_to_all(outgoing, 'beam', split_axis=0, concat_axis=0, tiled=True)  61.9 us
    gather x4, local copies, waits for them, and re-layouts, cut_window(): lax.dynamic_slice_in_dim(padded, (first_block - lowest_block) * BLK, wind...  15.9 us
    ppermute x4, starting transfers between devices, partner(): return lax.ppermute(block, axis, route)  11 us
    ppermute x2, waiting for transfers between devices, extended(): lax.ppermute(head, axis, [((i + 1) % count, i) for i in range(ends)])  9.07 us
    ppermute x2, starting transfers between devices, extended(): lax.ppermute(tail, axis, [(i, (i + 1) % count) for i in range(ends)])  8.89 us
    slice x2, local copies, waits for them, and re-layouts, interpolate(): windows[:, 1]  4.35 us
    slice x2, local copies, waits for them, and re-layouts, interpolate(): windows[:, 0]  4.17 us
    ppermute x2, starting transfers between devices, extended(): lax.ppermute(head, axis, [((i + 1) % count, i) for i in range(ends)])  3.96 us
  transfers between devices with their start and end apart: 8, of which 5 were waited for; matrix products, arithmetic and copies ran while one was open for 29% of the time, Pallas kernels for 0%

commit v1 on v0

v1 whole, which is shorter than its diff:
```python
import jax
import jax.numpy as jnp
from jax import lax
from jax.experimental import pallas as pl
from jax.experimental.pallas import tpu as pltpu
from jax.sharding import PartitionSpec as P

BLK = 32
WIN = 320
PS = 128
OS = 64
NW = 10
RIM_BLK = 6
Q = 128
MESH = pl.DeviceIdType.MESH
BF16 = jnp.bfloat16
F32 = jnp.float32


def complex_product(left, right, rows):
    p = jnp.dot(left, right, preferred_element_type=F32)
    return p[:rows, :Q] - p[rows:, Q:], p[:rows, Q:] + p[rows:, :Q]


def kernel(
    sub, kern, w0h, w1h, st0, st1, own, out,
    x, kc, w0t, w1t, w0, w1, r0a, r0b, r0c, r0d, s0, q0, l1a, l1b, sx, rx, yo, qq, og,
    in_sem, k_sem, r_ssem, r_rsem, q_ssem, q_rsem, l_ssem, l_rsem, x_ssem, x_rsem, a_ssem, a_rsem, o_sem,
):
    ap = lax.axis_index("aperture")
    z = lax.axis_index("beam")
    n_beam = lax.axis_size("beam")
    h = lax.rem(ap, 2)
    t = lax.rem(ap // 2, 2)
    up = (ap, lax.rem(z + 1, n_beam))
    down = (ap, lax.rem(z + n_beam - 1, n_beam))
    core = (ap + 1 - 2 * h, z)
    across = (ap + 2 - 4 * t, z)
    first = z == 0
    last = z == n_beam - 1
    beams = x.shape[1]
    blocks0 = beams // BLK
    parts = [(1 - h) * 2 + 1 - t, h * 2 + 1 - t, (1 - h) * 2 + t, h * 2 + t]

    r0 = (r0a, r0b, r0c, r0d)
    l1 = (l1a, l1b)

    loads = [pltpu.make_async_copy(sub.at[0], x, in_sem.at[0])]
    loads[0].start()
    kloads = []
    for i in range(4):
        cols = pl.ds(pl.multiple_of(parts[i] * Q, Q), Q)
        for c in range(2):
            cp = pltpu.make_async_copy(kern.at[0, c, :, cols], kc.at[i, :, pl.ds(c * Q, Q)], k_sem.at[2 * i + c])
            cp.start()
            kloads.append(cp)
    for k, (src, dst) in enumerate(((w0h, w0t), (w1h, w1t))):
        cp = pltpu.make_async_copy(src.at[0], dst, in_sem.at[1 + k])
        cp.start()
        loads.append(cp)

    barrier = pltpu.get_barrier_semaphore()
    peers = [(ap, lax.rem(z + k, n_beam)) for k in range(1, n_beam)] + [core, across]
    for peer in peers:
        pl.semaphore_signal(barrier, inc=1, device_id=peer, device_id_type=MESH)

    def send(src, dst, ssem, rsem, peer):
        cp = pltpu.make_async_remote_copy(src, dst, ssem, rsem, device_id=peer, device_id_type=MESH)
        cp.start()
        return cp

    def rims(buf, i, blocks, ssem, rsem):
        low = send(buf[i].at[pl.ds(RIM_BLK, RIM_BLK)], buf[i].at[pl.ds(RIM_BLK + blocks, RIM_BLK)], ssem.at[i, 0], rsem.at[i, 0], down)
        high = send(buf[i].at[pl.ds(blocks, RIM_BLK)], buf[i].at[pl.ds(0, RIM_BLK)], ssem.at[i, 1], rsem.at[i, 1], up)
        return [low, high]

    def clear_ends(buf, i, blocks):
        @pl.when(first)
        def _():
            buf[i][pl.ds(0, RIM_BLK)] = jnp.zeros((RIM_BLK, BLK, 2 * Q), BF16)

        @pl.when(last)
        def _():
            buf[i][pl.ds(RIM_BLK + blocks, RIM_BLK)] = jnp.zeros((RIM_BLK, BLK, 2 * Q), BF16)

    r_cps = []
    loads[0].wait()
    for i in range(4):
        kloads[2 * i].wait()
        kloads[2 * i + 1].wait()
        re, im = complex_product(x[...].reshape(2 * beams, x.shape[2]), kc[i], beams)
        r0[i][pl.ds(RIM_BLK, blocks0), :, pl.ds(0, Q)] = re.astype(BF16).reshape(blocks0, BLK, Q)
        r0[i][pl.ds(RIM_BLK, blocks0), :, pl.ds(Q, Q)] = im.astype(BF16).reshape(blocks0, BLK, Q)
        if i == 0:
            pl.semaphore_wait(barrier, len(peers))
        r_cps.append(rims(r0, i, blocks0, r_ssem, r_rsem))

    places = []
    none = jnp.int32(own.shape[0])
    for k in range(n_beam):
        d = lax.rem(z + k, n_beam)
        one = two = none
        for o in reversed(range(own.shape[0])):
            hit = own[o] == d
            two = jnp.where(hit, one, two)
            one = jnp.where(hit, jnp.int32(o), one)
        places.append((one, two))
    qq[own.shape[0]] = jnp.zeros((OS, 2 * Q), BF16)

    def window(starts, j, blocks):
        at = starts[j, ap] - (blocks * z - RIM_BLK)
        return jnp.minimum(jnp.maximum(at, 2 * j), 2 * j + 4)

    def turn(src, dst, lo, hi):
        for j in range(lo, hi):
            for c in range(2):
                dst[j, c] = src[j, c].T

    n0 = w0.shape[0]
    n1 = w1.shape[0]
    loads[1].wait()
    turn(w0t, w0, 0, n0)
    loads[2].wait()
    blocks1 = n0 * PS // BLK
    q_cps = []
    l_cps = []
    for i in range(4):
        r_cps[i][0].wait_recv()
        r_cps[i][1].wait_recv()
        clear_ends(r0, i, blocks0)
        u = i // 2
        if i % 2:
            q_cps[u].wait_recv()
        for j in range(n0):
            at = window(st0, j, blocks0)
            re, im = complex_product(w0[j].reshape(2 * PS, WIN), r0[i][pl.ds(at, NW)].reshape(WIN, 2 * Q), PS)
            rows = pl.ds(j * PS, PS)
            if i % 2 == 0:
                s0[u, rows, pl.ds(0, Q)] = re.astype(BF16)
                s0[u, rows, pl.ds(Q, Q)] = im.astype(BF16)
            else:
                to = pl.ds(RIM_BLK + j * PS // BLK, PS // BLK)
                for part, lanes in ((re, pl.ds(0, Q)), (im, pl.ds(Q, Q))):
                    both = part.astype(BF16).astype(F32) + q0[u, rows, lanes].astype(F32)
                    l1[u][to, :, lanes] = both.astype(BF16).reshape(PS // BLK, BLK, Q)
        if i % 2 == 0:
            q_cps.append(send(s0.at[u], q0.at[u], q_ssem.at[u], q_rsem.at[u], core))
        else:
            l_cps.append(rims(l1, u, blocks1, l_ssem, l_rsem))
        if i < 2:
            turn(w1t, w1, i * n1 // 2, (i + 1) * n1 // 2)

    x_cps = []
    for u in range(2):
        l_cps[u][0].wait_recv()
        l_cps[u][1].wait_recv()
        clear_ends(l1, u, blocks1)
        for j in range(n1):
            at = window(st1, j, blocks1)
            re, im = complex_product(w1[j].reshape(2 * PS, WIN), l1[u][pl.ds(at, NW)].reshape(WIN, 2 * Q), PS)
            rows = pl.ds(j * PS, PS)
            dst = yo if u else sx
            dst[rows, pl.ds(0, Q)] = re.astype(BF16)
            dst[rows, pl.ds(Q, Q)] = im.astype(BF16)
            if u == 0:
                x_cps.append(send(sx.at[rows], rx.at[rows], x_ssem.at[j], x_rsem.at[j], across))
    for j in range(n1):
        rows = pl.ds(j * PS, PS)
        x_cps[j].wait_recv()
        both = yo[rows, :].astype(F32) + rx[rows, :].astype(F32)
        qq[pl.ds(j * PS // OS, PS // OS)] = both.astype(BF16).reshape(PS // OS, OS, 2 * Q)

    mine = pl.ds(2 * z, 2)
    a_cps = []
    order = [n_beam // 2]
    for k in range(n_beam // 2 - 1, 0, -1):
        order += [k, n_beam - k]
    for n, k in enumerate(order + [0]):
        d = lax.rem(z + k, n_beam)
        for c in range(2):
            sector = qq[places[k][c]]
            og[2 * d + c, 0] = sector[:, :Q]
            og[2 * d + c, 1] = sector[:, Q:]
        if k:
            a_cps.append(send(og.at[pl.ds(2 * d, 2)], out.at[mine], a_ssem.at[n], a_rsem.at[n], (ap, d)))
    local = pltpu.make_async_copy(og.at[mine], out.at[mine], o_sem)
    local.start()
    local.wait()
    for cp in a_cps:
        cp.wait()
    for cp in [c for pair in r_cps + l_cps for c in pair] + q_cps + x_cps:
        cp.wait_send()


def local(subimages, range_kernel, weights0, starts0, weights1, starts1, owners):
    beams, rng = subimages.shape[2], subimages.shape[3]
    n0, n1 = weights0.shape[1], weights1.shape[1]
    n_own = owners.shape[1]
    n_beam = lax.axis_size("beam")
    slots = 2 * n_beam
    hbm = pl.BlockSpec(memory_space=pl.ANY)
    smem = pl.BlockSpec(memory_space=pltpu.SMEM)
    dma = pltpu.SemaphoreType.DMA
    merged = pl.pallas_call(
        kernel,
        out_shape=jax.ShapeDtypeStruct((slots, 2, OS, Q), BF16),
        in_specs=[hbm, hbm, hbm, hbm, smem, smem, smem],
        out_specs=pl.BlockSpec(memory_space=pltpu.VMEM),
        scratch_shapes=[
            pltpu.VMEM((2, beams, rng), BF16),
            pltpu.VMEM((4, rng, 2 * Q), BF16),
            pltpu.VMEM((n0, 2, WIN, PS), BF16),
            pltpu.VMEM((n1, 2, WIN, PS), BF16),
            pltpu.VMEM((n0, 2, PS, WIN), BF16),
            pltpu.VMEM((n1, 2, PS, WIN), BF16),
            pltpu.VMEM((beams // BLK + 2 * RIM_BLK, BLK, 2 * Q), BF16),
            pltpu.VMEM((beams // BLK + 2 * RIM_BLK, BLK, 2 * Q), BF16),
            pltpu.VMEM((beams // BLK + 2 * RIM_BLK, BLK, 2 * Q), BF16),
            pltpu.VMEM((beams // BLK + 2 * RIM_BLK, BLK, 2 * Q), BF16),
            pltpu.VMEM((2, n0 * PS, 2 * Q), BF16),
            pltpu.VMEM((2, n0 * PS, 2 * Q), BF16),
            pltpu.VMEM((n0 * PS // BLK + 2 * RIM_BLK, BLK, 2 * Q), BF16),
            pltpu.VMEM((n0 * PS // BLK + 2 * RIM_BLK, BLK, 2 * Q), BF16),
            pltpu.VMEM((n1 * PS, 2 * Q), BF16),
            pltpu.VMEM((n1 * PS, 2 * Q), BF16),
            pltpu.VMEM((n1 * PS, 2 * Q), BF16),
            pltpu.VMEM((n1 * PS // OS + 1, OS, 2 * Q), BF16),
            pltpu.VMEM((slots, 2, OS, Q), BF16),
            dma((3,)),
            dma((8,)),
            dma((4, 2)),
            dma((4, 2)),
            dma((2,)),
            dma((2,)),
            dma((2, 2)),
            dma((2, 2)),
            dma((n1,)),
            dma((n1,)),
            dma((n_beam - 1,)),
            dma((n_beam - 1,)),
            dma,
        ],
        compiler_params=pltpu.CompilerParams(collective_id=0, has_side_effects=True),
    )(
        subimages,
        range_kernel,
        jnp.swapaxes(weights0, 3, 4),
        jnp.swapaxes(weights1, 3, 4),
        starts0.T,
        starts1.T,
        owners.reshape(n_own),
    )
    return merged[None]


def solution(mesh):
    return jax.shard_map(
        local,
        mesh=mesh,
        in_specs=(
            P("aperture", None, "beam", None),
            P("aperture", None, None, None),
            P("aperture", "beam", None, None, None),
            P(None, "beam"),
            P("aperture", "beam", None, None, None),
            P(None, "beam"),
            P("aperture", "beam", None),
        ),
        out_specs=P("aperture", "beam", None, None, None),
        check_vma=False,
    )
```

time: 163 us -> 92.3 us (0.57)
  the two profiles are of different devices: /device:TPU:48 before, /device:TPU:1 now
where the time goes in v1:
time: 92.3 us; the launch traced here: 92.1 us
  Pallas kernels  89.8 us (97%)
  local copies, waits for them, and re-layouts  2.31 us (3%)
    pallas_call x1, Pallas kernels, local(): pl.pallas_call(kernel, out_shape=jax.ShapeDtypeStruct((slots, 2, OS, Q),...  89.8 us
    unnamed x1, local copies, waits for them, and re-layouts  2.31 us

profile of v1, /device:TPU:1, one launch (start us, length us, event | category | flops | bytes accessed | tf_op | source)
XLA Modules:
  0.0 92.1 jit_solution(17281338866945470710)
XLA Ops:
  0.0 89.8 %shard_map.73 = bf16[32,2,64,128]{3,2,1,0:T(8,128)(2,1)} custom-call(bf16[1,2,256,512]{3,2,1,0:T(8,128)(2,1)} %sub.1, bf16[1,2,512,512]{3,2,1,0:T(8,128)(2,1)} %kern.1, bf16[1,4,2,320,128]{4,3,2,1,0:T(8,128)(2,1)} %bitcast.8, bf16[1,8,2,320,128]{4,3,2,1,0:T(8,128)(2,1)} %bitcast.7, s32[4,32]{1,0:T(4,128)} %bitcast.10, s32[8,32]{1,0:T(8,128)} %bitcast.9, ...), custom_call_target="tpu_custom_call" | custom-call | tf_op jit(solution)/shard_map/pallas_call | solution.py:204
  89.8 2.3 %copy.9 = bf16[1,32,2,64,128]{4,3,2,1,0:T(8,128)(2,1)} copy(bf16[1,32,2,64,128]{4,3,2,1,0:T(8,128)(2,1)} %bitcast.6) | data formatting | bytes 2097152

commit v2 on v1

--- a/solution.py
+++ b/solution.py
@@ -24,8 +24,8 @@
 
 def kernel(
     sub, kern, w0h, w1h, st0, st1, own, out,
-    x, kc, w0t, w1t, w0, w1, r0a, r0b, r0c, r0d, s0, q0, l1a, l1b, sx, rx, yo, qq, og,
-    in_sem, k_sem, r_ssem, r_rsem, q_ssem, q_rsem, l_ssem, l_rsem, x_ssem, x_rsem, a_ssem, a_rsem, o_sem,
+    x, kc, w0t, w1t, w0, w1, r0a, r0b, r0c, r0d, s0, q0, l1a, l1b, sx, rx, px, yo, og, other,
+    in_sem, k_sem, r_ssem, r_rsem, q_ssem, q_rsem, l_ssem, l_rsem, x_ssem, x_rsem, a_ssem, a_rsem, o_sem, o_ssem, o_rsem,
 ):
     ap = lax.axis_index("aperture")
     z = lax.axis_index("beam")
@@ -93,19 +93,32 @@
         r0[i][pl.ds(RIM_BLK, blocks0), :, pl.ds(Q, Q)] = im.astype(BF16).reshape(blocks0, BLK, Q)
         if i == 0:
             pl.semaphore_wait(barrier, len(peers))
+            o_cp = send(own, other, o_ssem, o_rsem, across)
         r_cps.append(rims(r0, i, blocks0, r_ssem, r_rsem))
 
-    places = []
-    none = jnp.int32(own.shape[0])
-    for k in range(n_beam):
-        d = lax.rem(z + k, n_beam)
-        one = two = none
-        for o in reversed(range(own.shape[0])):
-            hit = own[o] == d
-            two = jnp.where(hit, one, two)
-            one = jnp.where(hit, jnp.int32(o), one)
-        places.append((one, two))
-    qq[own.shape[0]] = jnp.zeros((OS, 2 * Q), BF16)
+    order = [n_beam // 2]
+    for k in range(n_beam // 2 - 1, 0, -1):
+        order += [k, n_beam - k]
+    order.append(0)
+    n_own = own.shape[0]
+
+    def places(row):
+        table = []
+        for k in order:
+            d = lax.rem(z + k, n_beam)
+            one = two = jnp.int32(n_own)
+            for o in reversed(range(n_own)):
+                hit = row[o] == d
+                two = jnp.where(hit, one, two)
+                one = jnp.where(hit, jnp.int32(o), one)
+            table.append((one, two))
+        return table
+
+    own_places = places(own)
+    o_cp.wait_recv()
+    across_places = places(other)
+    for buf in (px, yo):
+        buf[n_own] = jnp.zeros((OS, 2 * Q), BF16)
 
     def window(starts, j, blocks):
         at = starts[j, ap] - (blocks * z - RIM_BLK)
@@ -155,30 +168,26 @@
         l_cps[u][0].wait_recv()
         l_cps[u][1].wait_recv()
         clear_ends(l1, u, blocks1)
+        dst = yo if u else px
         for j in range(n1):
             at = window(st1, j, blocks1)
             re, im = complex_product(w1[j].reshape(2 * PS, WIN), l1[u][pl.ds(at, NW)].reshape(WIN, 2 * Q), PS)
-            rows = pl.ds(j * PS, PS)
-            dst = yo if u else sx
-            dst[rows, pl.ds(0, Q)] = re.astype(BF16)
-            dst[rows, pl.ds(Q, Q)] = im.astype(BF16)
-            if u == 0:
-                x_cps.append(send(sx.at[rows], rx.at[rows], x_ssem.at[j], x_rsem.at[j], across))
-    for j in range(n1):
-        rows = pl.ds(j * PS, PS)
-        x_cps[j].wait_recv()
-        both = yo[rows, :].astype(F32) + rx[rows, :].astype(F32)
-        qq[pl.ds(j * PS // OS, PS // OS)] = both.astype(BF16).reshape(PS // OS, OS, 2 * Q)
+            sectors = pl.ds(j * PS // OS, PS // OS)
+            dst[sectors, :, pl.ds(0, Q)] = re.astype(BF16).reshape(PS // OS, OS, Q)
+            dst[sectors, :, pl.ds(Q, Q)] = im.astype(BF16).reshape(PS // OS, OS, Q)
+        if u == 0:
+            for n in range(n_beam):
+                for c in range(2):
+                    sx[n, c] = px[across_places[n][c]]
+                x_cps.append(send(sx.at[n], rx.at[n], x_ssem.at[n], x_rsem.at[n], across))
 
     mine = pl.ds(2 * z, 2)
     a_cps = []
-    order = [n_beam // 2]
-    for k in range(n_beam // 2 - 1, 0, -1):
-        order += [k, n_beam - k]
-    for n, k in enumerate(order + [0]):
+    for n, k in enumerate(order):
         d = lax.rem(z + k, n_beam)
+        x_cps[n].wait_recv()
         for c in range(2):
-            sector = qq[places[k][c]]
+            sector = (yo[own_places[n][c]].astype(F32) + rx[n, c].astype(F32)).astype(BF16)
             og[2 * d + c, 0] = sector[:, :Q]
             og[2 * d + c, 1] = sector[:, Q:]
         if k:
@@ -188,6 +197,7 @@
     local.wait()
     for cp in a_cps:
         cp.wait()
+    o_cp.wait_send()
     for cp in [c for pair in r_cps + l_cps for c in pair] + q_cps + x_cps:
         cp.wait_send()
 
@@ -221,11 +231,12 @@
             pltpu.VMEM((2, n0 * PS, 2 * Q), BF16),
             pltpu.VMEM((n0 * PS // BLK + 2 * RIM_BLK, BLK, 2 * Q), BF16),
             pltpu.VMEM((n0 * PS // BLK + 2 * RIM_BLK, BLK, 2 * Q), BF16),
-            pltpu.VMEM((n1 * PS, 2 * Q), BF16),
-            pltpu.VMEM((n1 * PS, 2 * Q), BF16),
-            pltpu.VMEM((n1 * PS, 2 * Q), BF16),
-            pltpu.VMEM((n1 * PS // OS + 1, OS, 2 * Q), BF16),
+            pltpu.VMEM((n_beam, 2, OS, 2 * Q), BF16),
+            pltpu.VMEM((n_beam, 2, OS, 2 * Q), BF16),
+            pltpu.VMEM((n_own + 1, OS, 2 * Q), BF16),
+            pltpu.VMEM((n_own + 1, OS, 2 * Q), BF16),
             pltpu.VMEM((slots, 2, OS, Q), BF16),
+            pltpu.SMEM((n_own,), jnp.int32),
             dma((3,)),
             dma((8,)),
             dma((4, 2)),
@@ -234,10 +245,12 @@
             dma((2,)),
             dma((2, 2)),
             dma((2, 2)),
-            dma((n1,)),
-            dma((n1,)),
+            dma((n_beam,)),
+            dma((n_beam,)),
             dma((n_beam - 1,)),
             dma((n_beam - 1,)),
+            dma,
+            dma,
             dma,
         ],
         compiler_params=pltpu.CompilerParams(collective_id=0, has_side_effects=True),

time: 92.3 us -> 84.3 us (0.913)
  Pallas kernels: 89.8 us -> 81.8 us
    pallas_call x1, Pallas kernels: 89.8 us -> 81.8 us  [local(): pl.pallas_call(kernel, out_shape=jax.ShapeDtypeStruct((slots, 2, OS, Q),...]
where the time goes in v2:
time: 84.3 us; the launch traced here: 84.1 us
  Pallas kernels  81.8 us (97%)
  local copies, waits for them, and re-layouts  2.31 us (3%)
    pallas_call x1, Pallas kernels, local(): pl.pallas_call(kernel, out_shape=jax.ShapeDtypeStruct((slots, 2, OS, Q),...  81.8 us
    unnamed x1, local copies, waits for them, and re-layouts  2.31 us

profile of v2, /device:TPU:1, one launch (start us, length us, event | category | flops | bytes accessed | tf_op | source)
XLA Modules:
  0.0 84.1 jit_solution(15274075455374442962)
XLA Ops:
  0.0 81.8 %shard_map.73 = bf16[32,2,64,128]{3,2,1,0:T(8,128)(2,1)} custom-call(bf16[1,2,256,512]{3,2,1,0:T(8,128)(2,1)} %sub.1, bf16[1,2,512,512]{3,2,1,0:T(8,128)(2,1)} %kern.1, bf16[1,4,2,320,128]{4,3,2,1,0:T(8,128)(2,1)} %bitcast.8, bf16[1,8,2,320,128]{4,3,2,1,0:T(8,128)(2,1)} %bitcast.7, s32[4,32]{1,0:T(4,128)} %bitcast.10, s32[8,32]{1,0:T(8,128)} %bitcast.9, ...), custom_call_target="tpu_custom_call" | custom-call | tf_op jit(solution)/shard_map/pallas_call | solution.py:214
  81.8 2.3 %copy.9 = bf16[1,32,2,64,128]{4,3,2,1,0:T(8,128)(2,1)} copy(bf16[1,32,2,64,128]{4,3,2,1,0:T(8,128)(2,1)} %bitcast.6) | data formatting | bytes 2097152

commit v3 on v2

--- a/solution.py
+++ b/solution.py
@@ -23,9 +23,9 @@
 
 
 def kernel(
-    sub, kern, w0h, w1h, st0, st1, own, out,
-    x, kc, w0t, w1t, w0, w1, r0a, r0b, r0c, r0d, s0, q0, l1a, l1b, sx, rx, px, yo, og, other,
-    in_sem, k_sem, r_ssem, r_rsem, q_ssem, q_rsem, l_ssem, l_rsem, x_ssem, x_rsem, a_ssem, a_rsem, o_sem, o_ssem, o_rsem,
+    sub, kern, w0h, w1h, st0h, st1h, ownh, out,
+    x, kc, w0t, w1t, w0, w1, r0a, r0b, r0c, r0d, s0, q0, l1a, l1b, sx, rx, px, yo, og, st0, st1, own, other,
+    in_sem, k_sem, r_ssem, r_rsem, q_ssem, q_rsem, l_ssem, l_rsem, x_ssem, x_rsem, a_ssem, a_rsem, o_sem, o_ssem, o_rsem, ring_sem,
 ):
     ap = lax.axis_index("aperture")
     z = lax.axis_index("beam")
@@ -45,6 +45,11 @@
     r0 = (r0a, r0b, r0c, r0d)
     l1 = (l1a, l1b)
 
+    barrier = pltpu.get_barrier_semaphore()
+    peers = [down, up, core, across]
+    for peer in peers:
+        pl.semaphore_signal(barrier, inc=1, device_id=peer, device_id_type=MESH)
+
     loads = [pltpu.make_async_copy(sub.at[0], x, in_sem.at[0])]
     loads[0].start()
     kloads = []
@@ -52,17 +57,19 @@
         cols = pl.ds(pl.multiple_of(parts[i] * Q, Q), Q)
         for c in range(2):
             cp = pltpu.make_async_copy(kern.at[0, c, :, cols], kc.at[i, :, pl.ds(c * Q, Q)], k_sem.at[2 * i + c])
-            cp.start()
             kloads.append(cp)
+    for cp in kloads[:2]:
+        cp.start()
     for k, (src, dst) in enumerate(((w0h, w0t), (w1h, w1t))):
-        cp = pltpu.make_async_copy(src.at[0], dst, in_sem.at[1 + k])
-        cp.start()
-        loads.append(cp)
-
-    barrier = pltpu.get_barrier_semaphore()
-    peers = [(ap, lax.rem(z + k, n_beam)) for k in range(1, n_beam)] + [core, across]
-    for peer in peers:
-        pl.semaphore_signal(barrier, inc=1, device_id=peer, device_id_type=MESH)
+        loads.append(pltpu.make_async_copy(src.at[0], dst, in_sem.at[1 + k]))
+    tables = []
+    for k, (src, dst) in enumerate(((ownh, own), (st0h, st0), (st1h, st1))):
+        tables.append(pltpu.make_async_copy(src, dst, in_sem.at[3 + k]))
+        tables[k].start()
+
+    def announce(r):
+        for k in (1 << r, n_beam - (1 << r)):
+            pl.semaphore_signal(ring_sem.at[r], inc=1, device_id=(ap, lax.rem(z + k, n_beam)), device_id_type=MESH)
 
     def send(src, dst, ssem, rsem, peer):
         cp = pltpu.make_async_remote_copy(src, dst, ssem, rsem, device_id=peer, device_id_type=MESH)
@@ -88,12 +95,16 @@
     for i in range(4):
         kloads[2 * i].wait()
         kloads[2 * i + 1].wait()
+        if i == 0:
+            for cp in kloads[2:] + loads[1:]:
+                cp.start()
         re, im = complex_product(x[...].reshape(2 * beams, x.shape[2]), kc[i], beams)
         r0[i][pl.ds(RIM_BLK, blocks0), :, pl.ds(0, Q)] = re.astype(BF16).reshape(blocks0, BLK, Q)
         r0[i][pl.ds(RIM_BLK, blocks0), :, pl.ds(Q, Q)] = im.astype(BF16).reshape(blocks0, BLK, Q)
         if i == 0:
             pl.semaphore_wait(barrier, len(peers))
-            o_cp = send(own, other, o_ssem, o_rsem, across)
+            announce(0)
+            o_cp = send(ownh, other, o_ssem, o_rsem, across)
         r_cps.append(rims(r0, i, blocks0, r_ssem, r_rsem))
 
     order = [n_beam // 2]
@@ -114,6 +125,8 @@
             table.append((one, two))
         return table
 
+    for cp in tables:
+        cp.wait()
     own_places = places(own)
     o_cp.wait_recv()
     across_places = places(other)
@@ -161,6 +174,8 @@
         else:
             l_cps.append(rims(l1, u, blocks1, l_ssem, l_rsem))
         if i < 2:
+            pl.semaphore_wait(ring_sem.at[i], 2)
+            announce(i + 1)
             turn(w1t, w1, i * n1 // 2, (i + 1) * n1 // 2)
 
     x_cps = []
@@ -180,6 +195,8 @@
                 for c in range(2):
                     sx[n, c] = px[across_places[n][c]]
                 x_cps.append(send(sx.at[n], rx.at[n], x_ssem.at[n], x_rsem.at[n], across))
+
+    pl.semaphore_wait(ring_sem.at[2], 2)
 
     mine = pl.ds(2 * z, 2)
     a_cps = []
@@ -209,12 +226,11 @@
     n_beam = lax.axis_size("beam")
     slots = 2 * n_beam
     hbm = pl.BlockSpec(memory_space=pl.ANY)
-    smem = pl.BlockSpec(memory_space=pltpu.SMEM)
     dma = pltpu.SemaphoreType.DMA
     merged = pl.pallas_call(
         kernel,
-        out_shape=jax.ShapeDtypeStruct((slots, 2, OS, Q), BF16),
-        in_specs=[hbm, hbm, hbm, hbm, smem, smem, smem],
+        out_shape=pltpu.VMEM((slots, 2, OS, Q), BF16),
+        in_specs=[hbm] * 7,
         out_specs=pl.BlockSpec(memory_space=pltpu.VMEM),
         scratch_shapes=[
             pltpu.VMEM((2, beams, rng), BF16),
@@ -236,8 +252,11 @@
             pltpu.VMEM((n_own + 1, OS, 2 * Q), BF16),
             pltpu.VMEM((n_own + 1, OS, 2 * Q), BF16),
             pltpu.VMEM((slots, 2, OS, Q), BF16),
+            pltpu.SMEM(starts0.shape[::-1], jnp.int32),
+            pltpu.SMEM(starts1.shape[::-1], jnp.int32),
             pltpu.SMEM((n_own,), jnp.int32),
-            dma((3,)),
+            pltpu.SMEM((n_own,), jnp.int32),
+            dma((6,)),
             dma((8,)),
             dma((4, 2)),
             dma((4, 2)),
@@ -252,6 +271,7 @@
             dma,
             dma,
             dma,
+            pltpu.SemaphoreType.REGULAR((3,)),
         ],
         compiler_params=pltpu.CompilerParams(collective_id=0, has_side_effects=True),
     )(

time: 84.3 us -> 77.7 us (0.922)
  Pallas kernels: 81.8 us -> 76.6 us
  local copies, waits for them, and re-layouts: 2.31 us -> 0.97 us
    pallas_call x1, Pallas kernels: 81.8 us -> 76.6 us  [local(): pl.pallas_call(kernel, out_shape=pltpu.VMEM((slots, 2, OS, Q), BF16), in_...]
    unnamed x1, local copies, waits for them, and re-layouts: 2.31 us -> 0.97 us
where the time goes in v3:
time: 77.7 us; the launch traced here: 77.5 us
  Pallas kernels  76.6 us (99%)
  local copies, waits for them, and re-layouts  0.97 us (1%)
    pallas_call x1, Pallas kernels, local(): pl.pallas_call(kernel, out_shape=pltpu.VMEM((slots, 2, OS, Q), BF16), in_...  76.6 us

profile of v3, /device:TPU:1, one launch (start us, length us, event | category | flops | bytes accessed | tf_op | source)
XLA Modules:
  0.0 77.5 jit_solution(1554870814200453872)
XLA Ops:
  0.0 76.6 %shard_map.73 = bf16[32,2,64,128]{3,2,1,0:T(8,128)(2,1)S(1)} custom-call(bf16[1,2,256,512]{3,2,1,0:T(8,128)(2,1)} %sub.1, bf16[1,2,512,512]{3,2,1,0:T(8,128)(2,1)} %kern.1, bf16[1,4,2,320,128]{4,3,2,1,0:T(8,128)(2,1)} %bitcast.8, bf16[1,8,2,320,128]{4,3,2,1,0:T(8,128)(2,1)} %bitcast.7, s32[4,32]{1,0:T(4,128)} %bitcast.10, s32[8,32]{1,0:T(8,128)} %bitcast.9, ...), custom_call_target="tpu_custom_call" | custom-call | tf_op jit(solution)/shard_map/pallas_call | solution.py:230
  76.6 1.0 %copy.9 = bf16[1,32,2,64,128]{4,3,2,1,0:T(8,128)(2,1)} copy(bf16[1,32,2,64,128]{4,3,2,1,0:T(8,128)(2,1)S(1)} %bitcast.6) | data formatting | bytes 2097152

commit v4 on v3

--- a/solution.py
+++ b/solution.py
@@ -38,6 +38,8 @@
     across = (ap + 2 - 4 * t, z)
     first = z == 0
     last = z == n_beam - 1
+    below = z > 0
+    above = z < n_beam - 1
     beams = x.shape[1]
     blocks0 = beams // BLK
     parts = [(1 - h) * 2 + 1 - t, h * 2 + 1 - t, (1 - h) * 2 + t, h * 2 + t]
@@ -46,9 +48,20 @@
     l1 = (l1a, l1b)
 
     barrier = pltpu.get_barrier_semaphore()
-    peers = [down, up, core, across]
-    for peer in peers:
-        pl.semaphore_signal(barrier, inc=1, device_id=peer, device_id_type=MESH)
+
+    def signal(sem, peer):
+        pl.semaphore_signal(sem, inc=1, device_id=peer, device_id_type=MESH)
+
+    def pair(k, act):
+        pl.when(z + k < n_beam)(lambda: act((ap, lax.rem(z + k, n_beam))))
+        pl.when(z >= k)(lambda: act((ap, lax.rem(z + n_beam - k, n_beam))))
+
+    def pair_count(k):
+        return jnp.where(z + k < n_beam, 1, 0) + jnp.where(z >= k, 1, 0)
+
+    signal(barrier, core)
+    signal(barrier, across)
+    pair(1, lambda peer: signal(barrier, peer))
 
     loads = [pltpu.make_async_copy(sub.at[0], x, in_sem.at[0])]
     loads[0].start()
@@ -68,8 +81,10 @@
         tables[k].start()
 
     def announce(r):
-        for k in (1 << r, n_beam - (1 << r)):
-            pl.semaphore_signal(ring_sem.at[r], inc=1, device_id=(ap, lax.rem(z + k, n_beam)), device_id_type=MESH)
+        pair(1 << r, lambda peer: signal(ring_sem.at[r], peer))
+
+    def heard(r):
+        pl.semaphore_wait(ring_sem.at[r], pair_count(1 << r))
 
     def send(src, dst, ssem, rsem, peer):
         cp = pltpu.make_async_remote_copy(src, dst, ssem, rsem, device_id=peer, device_id_type=MESH)
@@ -77,9 +92,29 @@
         return cp
 
     def rims(buf, i, blocks, ssem, rsem):
-        low = send(buf[i].at[pl.ds(RIM_BLK, RIM_BLK)], buf[i].at[pl.ds(RIM_BLK + blocks, RIM_BLK)], ssem.at[i, 0], rsem.at[i, 0], down)
-        high = send(buf[i].at[pl.ds(blocks, RIM_BLK)], buf[i].at[pl.ds(0, RIM_BLK)], ssem.at[i, 1], rsem.at[i, 1], up)
-        return [low, high]
+        def copy(src, dst, side, peer):
+            return pltpu.make_async_remote_copy(
+                buf[i].at[pl.ds(src, RIM_BLK)],
+                buf[i].at[pl.ds(dst, RIM_BLK)],
+                ssem.at[i, side],
+                rsem.at[i, side],
+                device_id=peer,
+                device_id_type=MESH,
+            )
+
+        low = copy(RIM_BLK, RIM_BLK + blocks, 0, down)
+        high = copy(blocks, 0, 1, up)
+        pl.when(below)(low.start)
+        pl.when(above)(high.start)
+        return low, high
+
+    def rims_in(cps):
+        pl.when(above)(cps[0].wait_recv)
+        pl.when(below)(cps[1].wait_recv)
+
+    def rims_out(cps):
+        pl.when(below)(cps[0].wait_send)
+        pl.when(above)(cps[1].wait_send)
 
     def clear_ends(buf, i, blocks):
         @pl.when(first)
@@ -102,10 +137,15 @@
         r0[i][pl.ds(RIM_BLK, blocks0), :, pl.ds(0, Q)] = re.astype(BF16).reshape(blocks0, BLK, Q)
         r0[i][pl.ds(RIM_BLK, blocks0), :, pl.ds(Q, Q)] = im.astype(BF16).reshape(blocks0, BLK, Q)
         if i == 0:
-            pl.semaphore_wait(barrier, len(peers))
+            pl.semaphore_wait(barrier, 2 + pair_count(1))
             announce(0)
             o_cp = send(ownh, other, o_ssem, o_rsem, across)
         r_cps.append(rims(r0, i, blocks0, r_ssem, r_rsem))
+        if i == 2:
+            heard(0)
+            announce(1)
+    heard(1)
+    announce(2)
 
     order = [n_beam // 2]
     for k in range(n_beam // 2 - 1, 0, -1):
@@ -151,8 +191,7 @@
     q_cps = []
     l_cps = []
     for i in range(4):
-        r_cps[i][0].wait_recv()
-        r_cps[i][1].wait_recv()
+        rims_in(r_cps[i])
         clear_ends(r0, i, blocks0)
         u = i // 2
         if i % 2:
@@ -174,14 +213,14 @@
         else:
             l_cps.append(rims(l1, u, blocks1, l_ssem, l_rsem))
         if i < 2:
-            pl.semaphore_wait(ring_sem.at[i], 2)
-            announce(i + 1)
+            if i == 0:
+                heard(2)
+                announce(3)
             turn(w1t, w1, i * n1 // 2, (i + 1) * n1 // 2)
 
     x_cps = []
     for u in range(2):
-        l_cps[u][0].wait_recv()
-        l_cps[u][1].wait_recv()
+        rims_in(l_cps[u])
         clear_ends(l1, u, blocks1)
         dst = yo if u else px
         for j in range(n1):
@@ -196,7 +235,7 @@
                     sx[n, c] = px[across_places[n][c]]
                 x_cps.append(send(sx.at[n], rx.at[n], x_ssem.at[n], x_rsem.at[n], across))
 
-    pl.semaphore_wait(ring_sem.at[2], 2)
+    heard(3)
 
     mine = pl.ds(2 * z, 2)
     a_cps = []
@@ -215,7 +254,9 @@
     for cp in a_cps:
         cp.wait()
     o_cp.wait_send()
-    for cp in [c for pair in r_cps + l_cps for c in pair] + q_cps + x_cps:
+    for cps in r_cps + l_cps:
+        rims_out(cps)
+    for cp in q_cps + x_cps:
         cp.wait_send()
 
 
@@ -271,7 +312,7 @@
             dma,
             dma,
             dma,
-            pltpu.SemaphoreType.REGULAR((3,)),
+            pltpu.SemaphoreType.REGULAR((4,)),
         ],
         compiler_params=pltpu.CompilerParams(collective_id=0, has_side_effects=True),
     )(

time: 77.7 us -> 76 us (0.978)
  Pallas kernels: 76.6 us -> 74.8 us
    pallas_call x1, Pallas kernels: 76.6 us -> 74.8 us  [local(): pl.pallas_call(kernel, out_shape=pltpu.VMEM((slots, 2, OS, Q), BF16), in_...]
where the time goes in v4:
time: 76 us; the launch traced here: 75.8 us
  Pallas kernels  74.8 us (98%)
  local copies, waits for them, and re-layouts  0.97 us (1%)
    pallas_call x1, Pallas kernels, local(): pl.pallas_call(kernel, out_shape=pltpu.VMEM((slots, 2, OS, Q), BF16), in_...  74.8 us

profile of v4, /device:TPU:1, one launch (start us, length us, event | category | flops | bytes accessed | tf_op | source)
XLA Modules:
  0.0 75.8 jit_solution(15151719742591674516)
XLA Ops:
  0.0 74.8 %shard_map.73 = bf16[32,2,64,128]{3,2,1,0:T(8,128)(2,1)S(1)} custom-call(bf16[1,2,256,512]{3,2,1,0:T(8,128)(2,1)} %sub.1, bf16[1,2,512,512]{3,2,1,0:T(8,128)(2,1)} %kern.1, bf16[1,4,2,320,128]{4,3,2,1,0:T(8,128)(2,1)} %bitcast.8, bf16[1,8,2,320,128]{4,3,2,1,0:T(8,128)(2,1)} %bitcast.7, s32[4,32]{1,0:T(4,128)} %bitcast.10, s32[8,32]{1,0:T(8,128)} %bitcast.9, ...), custom_call_target="tpu_custom_call" | custom-call | tf_op jit(solution)/shard_map/pallas_call | solution.py:271
  74.8 1.0 %copy.9 = bf16[1,32,2,64,128]{4,3,2,1,0:T(8,128)(2,1)} copy(bf16[1,32,2,64,128]{4,3,2,1,0:T(8,128)(2,1)S(1)} %bitcast.6) | data formatting | bytes 2097152

commit v5 on v4

--- a/solution.py
+++ b/solution.py
@@ -147,8 +147,11 @@
     heard(1)
     announce(2)
 
-    order = [n_beam // 2]
-    for k in range(n_beam // 2 - 1, 0, -1):
+    order = []
+    for k in range(n_beam // 2 - 1, n_beam // 4 - 1, -1):
+        order += [k, n_beam - k]
+    order.append(n_beam // 2)
+    for k in range(n_beam // 4 - 1, 0, -1):
         order += [k, n_beam - k]
     order.append(0)
     n_own = own.shape[0]

time: 76 us -> 76 us (level)
  no operation moved by 1% of the time
where the time goes in v5:
time: 76 us; the launch traced here: 75.9 us
  Pallas kernels  74.9 us (99%)
  local copies, waits for them, and re-layouts  0.97 us (1%)
    pallas_call x1, Pallas kernels, local(): pl.pallas_call(kernel, out_shape=pltpu.VMEM((slots, 2, OS, Q), BF16), in_...  74.9 us

profile of v5, /device:TPU:1, one launch (start us, length us, event | category | flops | bytes accessed | tf_op | source)
XLA Modules:
  0.0 75.9 jit_solution(13932469608226313148)
XLA Ops:
  0.0 74.9 %shard_map.73 = bf16[32,2,64,128]{3,2,1,0:T(8,128)(2,1)S(1)} custom-call(bf16[1,2,256,512]{3,2,1,0:T(8,128)(2,1)} %sub.1, bf16[1,2,512,512]{3,2,1,0:T(8,128)(2,1)} %kern.1, bf16[1,4,2,320,128]{4,3,2,1,0:T(8,128)(2,1)} %bitcast.8, bf16[1,8,2,320,128]{4,3,2,1,0:T(8,128)(2,1)} %bitcast.7, s32[4,32]{1,0:T(4,128)} %bitcast.10, s32[8,32]{1,0:T(8,128)} %bitcast.9, ...), custom_call_target="tpu_custom_call" | custom-call | tf_op jit(solution)/shard_map/pallas_call | solution.py:274
  74.9 1.0 %copy.9 = bf16[1,32,2,64,128]{4,3,2,1,0:T(8,128)(2,1)} copy(bf16[1,32,2,64,128]{4,3,2,1,0:T(8,128)(2,1)S(1)} %bitcast.6) | data formatting | bytes 2097152
